TPU v7x, 128 devices: a whole 4x4x4 slice. The times are simulated.
128 devices in a mesh: expert: 8 (over x, core), fsdp: 16 (over z, y).
Axes of the slice: x: 4, y: 4, z: 4, core: 2. Of those that a mesh axis runs over, the one named last changes fastest.
Arguments:
- tokens: bfloat16 [16384, 1536], P(('expert', 'fsdp')), may hold values from -6 to 6
- gate_probs: float32 [16384, 2], P(('expert', 'fsdp')), may hold values from 0.1 to 1
- expert_ids: int32 [16384, 2], P(('expert', 'fsdp')), may hold values from 0 to 7, all different within a row; in each aligned block of 128 rows (0 to 127, 128 to 255, ...) at most 32 rows name the same one
- cotangent: bfloat16 [16384, 1536], P(('expert', 'fsdp')), may hold values from -0.59765625 to 0.59765625
- gate_weight: bfloat16 [8, 1536, 2048], P('expert', None, 'fsdp'), may hold values from -0.15625 to 0.15625
- up_weight: bfloat16 [8, 1536, 2048], P('expert', None, 'fsdp'), may hold values from -0.15625 to 0.15625
- down_weight: bfloat16 [8, 2048, 1536], P('expert', 'fsdp'), may hold values from -0.125 to 0.125
Outputs:
- mixed: bfloat16 [16384, 1536], P(('expert', 'fsdp'))
- d_tokens: bfloat16 [16384, 1536], P(('expert', 'fsdp'))
- d_gates: float32 [16384, 2], P(('expert', 'fsdp'))
- d_gate_weight: float32 [8, 1536, 2048], P('expert', None, 'fsdp')
- d_up_weight: float32 [8, 1536, 2048], P('expert', None, 'fsdp')
- d_down_weight: float32 [8, 2048, 1536], P('expert', 'fsdp')
Inputs may be any that keep to these rules, and one draw needn't show every extreme that they name: `expert_ids`: the two experts of a token differ. In the 128 rows of one device every expert is named exactly 32 times.
All inputs are finite; a program needn't handle non-finite values.
Results may differ from a plain program's by a relative error of at most 0.015.
Values may be sent and summed in bfloat16 or wider, within the bound.
A program may use at most 192 MiB of HBM per device.

v0:
```python
import jax
import jax.numpy as jnp
from jax import lax
from jax.sharding import PartitionSpec as P


def build_dispatch(expert_ids, capacity, num_experts):
    flat_ids = expert_ids.reshape(-1)
    onehot = (flat_ids[:, None] == jnp.arange(num_experts, dtype=jnp.int32)[None, :]).astype(
        jnp.int32
    )
    before = jnp.cumsum(onehot, axis=0) - onehot
    slot_pos = jnp.sum(before * onehot, axis=1)
    target = flat_ids * capacity + slot_pos
    return (jnp.arange(num_experts * capacity, dtype=jnp.int32)[:, None] == target[None, :]).astype(
        jnp.bfloat16
    )


def deliver(buffer):
    arrived = lax.all_to_all(buffer, "expert", split_axis=0, concat_axis=0, tiled=True)
    arrived = lax.all_gather(arrived[None], "fsdp", axis=0, tiled=True)
    return arrived.reshape(-1, buffer.shape[-1])


def bring_back(partial_value, num_experts, capacity):
    columns = partial_value.shape[-1]
    blocks = partial_value.astype(jnp.bfloat16).reshape(-1, num_experts, capacity, columns)
    summed = lax.psum_scatter(blocks, "fsdp", scatter_dimension=0, tiled=True).astype(jnp.float32)
    result = lax.all_to_all(
        summed[0].astype(jnp.bfloat16), "expert", split_axis=0, concat_axis=0, tiled=True
    )
    return result.reshape(num_experts * capacity, columns)


def per_device(tokens, gate_probs, expert_ids, cotangent, gate_weight, up_weight, down_weight):
    tok_rows, columns = tokens.shape
    num_experts = lax.axis_size("expert")
    capacity = 2 * tok_rows // num_experts
    dispatch = build_dispatch(expert_ids, capacity, num_experts)
    token_map = jnp.sum(dispatch.reshape(num_experts * capacity, tok_rows, 2), axis=2)
    contract_rows = (((0,), (0,)), ((), ()))
    contract_cols = (((1,), (1,)), ((), ()))
    outgoing = jnp.dot(token_map, tokens, preferred_element_type=jnp.float32).astype(jnp.bfloat16)
    cot_wide = cotangent.astype(jnp.float32)
    scaled = (
        (gate_probs[:, :, None] * cot_wide[:, None, :])
        .astype(jnp.bfloat16)
        .reshape(2 * tok_rows, columns)
    )
    grad_out = jnp.dot(dispatch, scaled, preferred_element_type=jnp.float32).astype(jnp.bfloat16)
    token_slots = outgoing.reshape(num_experts, capacity, columns)
    grad_slots = grad_out.reshape(num_experts, capacity, columns)
    rows_in = deliver(token_slots)
    w_gate = gate_weight[0]
    w_up = up_weight[0]
    w_down = down_weight[0]
    pre_gate = jnp.dot(rows_in, w_gate, preferred_element_type=jnp.float32)
    pre_up = jnp.dot(rows_in, w_up, preferred_element_type=jnp.float32)
    sigmoid_gate = jax.nn.sigmoid(pre_gate)
    hidden = (pre_gate * sigmoid_gate * pre_up).astype(jnp.bfloat16)
    partial_value = jnp.dot(hidden, w_down, preferred_element_type=jnp.float32)
    expert_out = bring_back(partial_value, num_experts, capacity)
    per_pair = lax.dot_general(
        dispatch, expert_out, contract_rows, preferred_element_type=jnp.float32
    ).reshape(tok_rows, 2, columns)
    mixed = jnp.sum(gate_probs[:, :, None] * per_pair, axis=1).astype(jnp.bfloat16)
    d_gates = jnp.sum(cot_wide[:, None, :] * per_pair, axis=2)
    grad_rows = deliver(grad_slots)
    d_hidden = lax.dot_general(grad_rows, w_down, contract_cols, preferred_element_type=jnp.float32)
    d_pre_gate = (
        d_hidden * pre_up * sigmoid_gate * (1.0 + pre_gate * (1.0 - sigmoid_gate))
    ).astype(jnp.bfloat16)
    d_pre_up = (d_hidden * pre_gate * sigmoid_gate).astype(jnp.bfloat16)
    d_down = lax.dot_general(hidden, grad_rows, contract_rows, preferred_element_type=jnp.float32)
    d_gate_w = lax.dot_general(
        rows_in, d_pre_gate, contract_rows, preferred_element_type=jnp.float32
    )
    d_up_w = lax.dot_general(rows_in, d_pre_up, contract_rows, preferred_element_type=jnp.float32)
    back_partial = lax.dot_general(
        d_pre_gate, w_gate, contract_cols, preferred_element_type=jnp.float32
    )
    back_partial = back_partial + lax.dot_general(
        d_pre_up, w_up, contract_cols, preferred_element_type=jnp.float32
    )
    d_rows = bring_back(back_partial, num_experts, capacity)
    d_tokens = lax.dot_general(
        token_map, d_rows, contract_rows, preferred_element_type=jnp.float32
    ).astype(jnp.bfloat16)
    return (mixed, d_tokens, d_gates, d_gate_w[None], d_up_w[None], d_down[None])


def solution(mesh):
    placed = (
        P(("expert", "fsdp"), None),
        P(("expert", "fsdp"), None),
        P(("expert", "fsdp"), None),
        P(("expert", "fsdp"), None),
        P("expert", None, "fsdp"),
        P("expert", None, "fsdp"),
        P("expert", "fsdp", None),
    )
    return jax.shard_map(
        per_device,
        mesh=mesh,
        in_specs=placed,
        out_specs=(
            P(("expert", "fsdp"), None),
            P(("expert", "fsdp"), None),
            P(("expert", "fsdp"), None),
            P("expert", None, "fsdp"),
            P("expert", None, "fsdp"),
            P("expert", "fsdp", None),
        ),
        check_vma=False,
    )
```

profile of v0, /device:TPU:1, one launch (start us, length us, event | category | flops | bytes accessed | tf_op | source)
XLA Modules:
  0.0 466.0 jit_solution(14920518914551212987)
XLA Ops:
  7.2 0.0 all-gather.5.cloned.1.call-start
  7.2 0.9 copy.36
  8.1 0.1 reshape.107
  8.3 0.1 eq.62
  8.4 0.6 reduce-window.6
  9.0 0.2 slice_reduce_fusion
  9.3 0.1 fusion.17
  9.4 0.1 reduce_sum.42
  9.5 0.1 copy.38
  9.6 0.7 multiply_add_fusion
  10.3 0.6 copy-done.9
  10.9 1.3 convolution_convert_fusion.1
  12.3 17.8 %all_to_all.20 = bf16[8,32,1536]{2,1,0:T(8,128)(2,1)} all-to-all(bf16[8,32,1536]{2,1,0:T(8,128)(2,1)S(1)} %bitcast.70), channel_id=1, replica_groups=mesh['expert'=8,'fsdp'=16] {'expert'}, dimensions={0} | all-to-all | bytes 1572864 | tf_op jit(solution)/shard_map/all_to_all | solution.py:21
  30.1 0.0 all-gather.5.cloned.1.call-update
  30.1 0.0 all-gather.7.cloned.1.call-start
  30.2 0.1 copy.40
  30.3 0.1 mul.83
  30.5 0.4 mul.85.clone
  30.9 1.1 mul.86
  32.0 0.5 convolution_convert_fusion.2
  32.5 16.3 %all_to_all.21 = bf16[8,32,1536]{2,1,0:T(8,128)(2,1)} all-to-all(bf16[8,32,1536]{2,1,0:T(8,128)(2,1)S(1)} %bitcast.71), channel_id=1, replica_groups=mesh['expert'=8,'fsdp'=16] {'expert'}, dimensions={0} | all-to-all | bytes 1572864 | tf_op jit(solution)/shard_map/all_to_all | solution.py:21
  48.7 0.0 all-gather.7.cloned.1.call-update
  48.7 0.2 reduce-scatter.9.cloned.1.call-start
  49.0 72.0 %all-gather.5.cloned.1.call-done = bf16[128,32,1536]{2,1,0:T(8,128)(2,1)} async-done(((bf16[8,32,1536]{2,1,0:T(8,128)(2,1)}), bf16[128,32,1536]{2,1,0:T(8,128)(2,1)}) %all-gather.5.cloned.1.call-update) | async-done | bytes 12582928 | tf_op jit(solution)/shard_map/all_gather | solution.py:22
  120.9 7.9 %fusion.5 = f32[4096,128]{1,0:T(8,128)} fusion(bf16[4096,1536]{1,0:T(8,128)(2,1)} %bitcast.63, bf16[1,1536,128]{2,1,0:T(8,128)(2,1)S(1)} %copy-done.2), kind=kOutput, calls=%fused_computation.20 | convolution fusion | flops 1610612736 | bytes 15073280 | tf_op jit(solution)/shard_map/dot_general | solution.py:59
  128.8 1.1 copy-done.1
  129.9 4.8 %fusion.9 = f32[4096,128]{1,0:T(8,128)} fusion(bf16[4096,1536]{1,0:T(8,128)(2,1)S(1)} %bitcast.66, bf16[1,1536,128]{2,1,0:T(8,128)(2,1)S(1)} %copy-done.5), kind=kOutput, calls=%fused_computation.24 | convolution fusion | flops 1610612736 | bytes 15073280 | tf_op jit(solution)/shard_map/dot_general | solution.py:58
  134.6 78.0 %all-gather.7.cloned.1.call-done = bf16[128,32,1536]{2,1,0:T(8,128)(2,1)} async-done(((bf16[8,32,1536]{2,1,0:T(8,128)(2,1)}), bf16[128,32,1536]{2,1,0:T(8,128)(2,1)}) %all-gather.7.cloned.1.call-update) | async-done | bytes 12582928 | tf_op jit(solution)/shard_map/all_gather | solution.py:22
  212.6 9.6 %multiply_convert_fusion = (bf16[4096,128]{1,0:T(8,128)(2,1)S(1)}, bf16[4096,128]{1,0:T(8,128)(2,1)S(1)}, bf16[4096,128]{1,0:T(8,128)(2,1)S(1)}) fusion(f32[4096,128]{1,0:T(8,128)} %fusion.9, f32[4096,128]{1,0:T(8,128)} %fusion.5, bf16[4096,1536]{1,0:T(8,128)(2,1)} %bitcast.67, bf16[1,128,1536]{2,1,0:T(8,128)(2,1)S(1)} %copy-done), kind=kOutput, calls=%fused_computation.8 | convolution fusion | flops 1619001344 | bytes 20316160 | tf_op jit(solution)/shard_map/dot_general | solution.py:70
  222.2 10.1 %fusion.7 = f32[4096,1536]{1,0:T(8,128)} fusion(bf16[4096,128]{1,0:T(8,128)(2,1)S(1)} %get-tuple-element.9, bf16[1,1536,128]{2,1,0:T(8,128)(2,1)S(1)} %copy-done.5), kind=kOutput, calls=%fused_computation.22 | convolution fusion | flops 1610612736 | bytes 26607616 | tf_op jit(solution)/shard_map/dot_general | solution.py:80
  232.4 14.7 %add_convert_fusion = bf16[4096,1536]{1,0:T(8,128)(2,1)} fusion(f32[4096,1536]{1,0:T(8,128)} %fusion.7, bf16[4096,128]{1,0:T(8,128)(2,1)S(1)} %get-tuple-element.8, bf16[1,1536,128]{2,1,0:T(8,128)(2,1)S(1)} %copy-done.2), kind=kOutput, calls=%fused_computation | convolution fusion | flops 1623195648 | bytes 39190528 | tf_op jit(solution)/shard_map/dot_general | solution.py:83
  247.1 0.0 reduce-scatter.9.cloned.1.call-update
  247.1 0.3 reduce-scatter.7.cloned.1.call-start
  247.4 6.4 %convolution_convert_fusion = bf16[4096,1536]{1,0:T(8,128)(2,1)} fusion(bf16[4096,128]{1,0:T(8,128)(2,1)S(1)} %get-tuple-element.10, bf16[1,128,1536]{2,1,0:T(8,128)(2,1)S(1)} %copy-done), kind=kOutput, calls=%fused_computation.1 | convolution fusion | flops 1616904192 | bytes 14024704 | tf_op jit(solution)/shard_map/dot_general | solution.py:62
  253.7 1.0 copy-done.4
  254.7 1.0 convert_element_type.65
  255.7 0.1 iota_compare_fusion.2
  255.8 0.7 eq.68
  256.5 7.5 %convolution_bitcast_fusion.1 = f32[1,1536,128]{2,1,0:T(8,128)} fusion(bf16[4096,1536]{1,0:T(8,128)(2,1)} %bitcast.64, bf16[4096,128]{1,0:T(8,128)(2,1)S(1)} %get-tuple-element.8), kind=kOutput, calls=%fused_computation.5 | convolution fusion | flops 1610612736 | bytes 14417920 | tf_op jit(solution)/shard_map/dot_general | solution.py:79
  264.0 77.9 %reduce-scatter.9.cloned.1.call-done = bf16[1,8,32,1536]{3,2,1,0:T(8,128)(2,1)} async-done(((bf16[16,8,32,1536]{3,2,1,0:T(8,128)(2,1)}), bf16[1,8,32,1536]{3,2,1,0:T(8,128)(2,1)}) %reduce-scatter.9.cloned.1.call-update) | async-done | bytes 786448
  341.9 5.4 %all-to-all-start.3 = ((bf16[8,32,1536]{2,1,0:T(8,128)(2,1)}), bf16[8,32,1536]{2,1,0:T(8,128)(2,1)S(1)}, u32[]{:S(2)}, u32[]{:S(2)}) async-start(bf16[8,32,1536]{2,1,0:T(8,128)(2,1)} %bitcast.73), calls=%async_computation.3 | async-start | bytes 1572864 | tf_op jit(solution)/shard_map/all_to_all | solution.py:30
  347.3 7.3 %convolution_bitcast_fusion.2 = f32[1,1536,128]{2,1,0:T(8,128)} fusion(bf16[4096,1536]{1,0:T(8,128)(2,1)} %bitcast.65, bf16[4096,128]{1,0:T(8,128)(2,1)S(1)} %copy-done.7), kind=kOutput, calls=%fused_computation.6 | convolution fusion | flops 1610612736 | bytes 14417920 | tf_op jit(solution)/shard_map/dot_general | solution.py:76
  354.6 84.7 %reduce-scatter.7.cloned.1.call-done = bf16[1,8,32,1536]{3,2,1,0:T(8,128)(2,1)} async-done(((bf16[16,8,32,1536]{3,2,1,0:T(8,128)(2,1)}), bf16[1,8,32,1536]{3,2,1,0:T(8,128)(2,1)}) %reduce-scatter.7.cloned.1.call-update) | async-done | bytes 786448
  439.4 5.4 %all-to-all-start.1 = ((bf16[8,32,1536]{2,1,0:T(8,128)(2,1)}), bf16[8,32,1536]{2,1,0:T(8,128)(2,1)}, u32[]{:S(2)}, u32[]{:S(2)}) async-start(bf16[8,32,1536]{2,1,0:T(8,128)(2,1)} %bitcast.72), calls=%async_computation.1 | async-start | bytes 1572864 | tf_op jit(solution)/shard_map/all_to_all | solution.py:30
  444.8 7.4 %convolution_bitcast_fusion = f32[1,128,1536]{2,1,0:T(8,128)} fusion(bf16[4096,128]{1,0:T(8,128)(2,1)S(1)} %get-tuple-element.10, bf16[4096,1536]{1,0:T(8,128)(2,1)} %bitcast.68), kind=kOutput, calls=%fused_computation.4 | convolution fusion | flops 1610612736 | bytes 14417920 | tf_op jit(solution)/shard_map/dot_general | solution.py:75
  452.2 1.0 convolution_convert_fusion.3
  453.2 3.8 all-to-all-done.1
  457.0 2.5 multiply_reduce_fusion
  (30 shorter events, 0.2 us)
Async XLA Ops:
  7.2 205.4 %copy-start = (bf16[1,128,1536]{2,1,0:T(8,128)(2,1)S(1)}, bf16[1,128,1536]{2,1,0:T(8,128)(2,1)}, u32[]{:S(2)}) copy-start(bf16[1,128,1536]{2,1,0:T(8,128)(2,1)} %param.13) | copy-start | bytes 1179652
  7.2 23.0 %copy-start.12 = (f32[128,2]{0,1:T(2,128)S(1)}, f32[128,2]{0,1:T(2,128)}, u32[]{:S(2)}) copy-start(f32[128,2]{0,1:T(2,128)} %param.8) | copy-start | bytes 3076
  7.2 23.3 %copy-start.3 = (bf16[128,1536]{1,0:T(8,128)(2,1)S(1)}, bf16[128,1536]{1,0:T(8,128)(2,1)}, u32[]{:S(2)}) copy-start(bf16[128,1536]{1,0:T(8,128)(2,1)} %param.10) | copy-start | bytes 1179652
  7.2 113.7 %all-gather.5.cloned.1.call-start = ((), (), s32[]{:S(2)}) async-start(), calls=%async_computation.6 | async-start | bytes 13369344 | tf_op jit(solution)/shard_map/all_gather | solution.py:22
  10.3 0.6 copy-start.9
  30.1 182.5 %all-gather.7.cloned.1.call-start = ((), (), s32[]{:S(2)}) async-start(), calls=%async_computation.7 | async-start | bytes 13369344 | tf_op jit(solution)/shard_map/all_gather | solution.py:22
  32.0 89.0 %copy-start.2 = (bf16[1,1536,128]{2,1,0:T(8,128)(2,1)S(1)}, bf16[1,1536,128]{2,1,0:T(8,128)(2,1)}, u32[]{:S(2)}) copy-start(bf16[1,1536,128]{2,1,0:T(8,128)(2,1)} %param.12) | copy-start | bytes 1179652
  48.7 293.1 %reduce-scatter.9.cloned.1.call-start = ((), (), s32[]{:S(2)}) async-start(), calls=%async_computation.9 | async-start | bytes 13369344
  120.9 8.9 %copy-start.1 = (bf16[128,32,1536]{2,1,0:T(8,128)(2,1)S(1)}, bf16[128,32,1536]{2,1,0:T(8,128)(2,1)}, u32[]{:S(2)}) copy-start(bf16[128,32,1536]{2,1,0:T(8,128)(2,1)} %all-gather.5.cloned.1.call-done) | copy-start | bytes 37748740
  120.9 8.9 %copy-start.5 = (bf16[1,1536,128]{2,1,0:T(8,128)(2,1)S(1)}, bf16[1,1536,128]{2,1,0:T(8,128)(2,1)}, u32[]{:S(2)}) copy-start(bf16[1,1536,128]{2,1,0:T(8,128)(2,1)} %param.11) | copy-start | bytes 1179652
  222.2 10.1 %copy-start.6 = (bf16[4096,128]{1,0:T(8,128)(2,1)}, bf16[4096,128]{1,0:T(8,128)(2,1)S(1)}, u32[]{:S(2)}) copy-start(bf16[4096,128]{1,0:T(8,128)(2,1)S(1)} %get-tuple-element.9) | copy-start | bytes 3145732
  247.1 192.3 %reduce-scatter.7.cloned.1.call-start = ((), (), s32[]{:S(2)}) async-start(), calls=%async_computation.8 | async-start | bytes 13369344
  253.7 1.0 copy-start.4
  256.5 90.8 %copy-start.7 = (bf16[4096,128]{1,0:T(8,128)(2,1)S(1)}, bf16[4096,128]{1,0:T(8,128)(2,1)}, u32[]{:S(2)}) copy-start(bf16[4096,128]{1,0:T(8,128)(2,1)} %copy-done.6) | copy-start | bytes 3145732
  341.9 97.5 %all-to-all-start.3 = ((bf16[8,32,1536]{2,1,0:T(8,128)(2,1)}), bf16[8,32,1536]{2,1,0:T(8,128)(2,1)S(1)}, u32[]{:S(2)}, u32[]{:S(2)}) async-start(bf16[8,32,1536]{2,1,0:T(8,128)(2,1)} %bitcast.73), calls=%async_computation.3 | async-start | bytes 1572864 | tf_op jit(solution)/shard_map/all_to_all | solution.py:30
  439.4 17.7 %all-to-all-start.1 = ((bf16[8,32,1536]{2,1,0:T(8,128)(2,1)}), bf16[8,32,1536]{2,1,0:T(8,128)(2,1)}, u32[]{:S(2)}, u32[]{:S(2)}) async-start(bf16[8,32,1536]{2,1,0:T(8,128)(2,1)} %bitcast.72), calls=%async_computation.1 | async-start | bytes 1572864 | tf_op jit(solution)/shard_map/all_to_all | solution.py:30
  444.8 7.4 %copy-start.10 = (bf16[256,128]{1,0:T(8,128)(2,1)S(1)}, bf16[256,128]{1,0:T(8,128)(2,1)}, u32[]{:S(2)}) copy-start(bf16[256,128]{1,0:T(8,128)(2,1)} %copy-done.9) | copy-start | bytes 196612
  444.8 12.3 %copy-start.8 = (f32[128,1536]{1,0:T(8,128)S(1)}, f32[128,1536]{1,0:T(8,128)}, u32[]{:S(2)}) copy-start(f32[128,1536]{1,0:T(8,128)} %convert_element_type.65) | copy-start | bytes 2359300
  444.8 12.3 %copy-start.11 = (pred[128,2,256]{2,1,0:T(4,128)(4,1)S(1)}, pred[128,2,256]{2,1,0:T(4,128)(4,1)}, u32[]{:S(2)}) copy-start(pred[128,2,256]{2,1,0:T(4,128)(4,1)} %eq.68) | copy-start | bytes 196612
Sparse Core Ops, SparseCore 0:
  30.3 90.6 all-gather.4
  123.1 89.4 all-gather.6
  247.2 94.6 reduce-scatter.8
  345.2 94.1 reduce-scatter.6
where the time goes:
time: 467 us; the launch traced here: 466 us
  waiting for transfers between devices  316 us (68%)
  matrix products  81 us (17%)
  blocking collectives  34.1 us (7%)
  between operations  13.9 us (3%)
  starting transfers between devices  11.4 us (2%)
  local copies, waits for them, and re-layouts  6.75 us (1%)
    unnamed x6, waiting for transfers between devices  163 us
    all_gather x2, waiting for transfers between devices, deliver(): arrived = lax.all_gather(arrived[None], 'fsdp', axis=0, tiled=True)  150 us
    all_to_all x2, blocking collectives, deliver(): lax.all_to_all(buffer, 'expert', split_axis=0, concat_axis=0, tiled=True)  34.1 us
    dot_general x1, matrix products, per_device(): lax.dot_general(d_pre_up, w_up, contract_cols, preferred_element_type=jnp...  14.7 us
    all_to_all x2, starting transfers between devices, bring_back(): lax.all_to_all(summed[0].astype(jnp.bfloat16), 'expert', split_axis=0, co...  10.8 us
    dot_general x1, matrix products, per_device(): lax.dot_general(d_pre_gate, w_gate, contract_cols, preferred_element_type...  10.1 us
    dot_general x1, matrix products, per_device(): lax.dot_general(grad_rows, w_down, contract_cols, preferred_element_type=...  9.6 us
  transfers between devices with their start and end apart: 6, of which 5 were waited for; matrix products, arithmetic and copies ran while one was open for 10% of the time, Pallas kernels for 0%

commit v1 on v0

--- a/solution.py
+++ b/solution.py
@@ -19,7 +19,9 @@
 
 def deliver(buffer):
     arrived = lax.all_to_all(buffer, "expert", split_axis=0, concat_axis=0, tiled=True)
-    arrived = lax.all_gather(arrived[None], "fsdp", axis=0, tiled=True)
+    arrived = jnp.concatenate(
+        lax.all_to_all(jnp.stack([arrived[None]] * lax.axis_size("fsdp")), "fsdp", 0, 0), axis=0
+    )
     return arrived.reshape(-1, buffer.shape[-1])
 
 

time: 467 us -> 650 us (1.39)
  blocking collectives: 34.1 us -> 163 us
  waiting for transfers between devices: 316 us -> 343 us
  local copies, waits for them, and re-layouts: 6.75 us -> 19.1 us
  starting transfers between devices: 11.4 us -> 22.2 us
    all_to_all x0 -> x2, waiting for transfers between devices: none -> 176 us  [the longest x1 166 us: deliver(): lax.all_to_all(jnp.stack([arrived[None]] * lax.axis_size('fsdp')), 'fsdp'...]
    all_gather x2 -> x0, waiting for transfers between devices: 150 us -> none  [deliver(): arrived = lax.all_gather(arrived[None], 'fsdp', axis=0, tiled=True)]
    all_to_all x0 -> x1, blocking collectives: none -> 147 us  [deliver(): lax.all_to_all(jnp.stack([arrived[None]] * lax.axis_size('fsdp')), 'fsdp'...]
    all_to_all x2 -> x1, blocking collectives: 34.1 us -> 15.5 us  [deliver(): lax.all_to_all(buffer, 'expert', split_axis=0, concat_axis=0, tiled=True)]
    another operation x1 -> x3, local copies, waits for them, and re-layouts: 0.01 us -> 13.4 us  [the longest x2 13.4 us: deliver(): jnp.stack([arrived[None]] * lax.axis_size('fsdp'))]
    all_to_all x0 -> x2, starting transfers between devices: none -> 10.9 us  [the longest x1 5.79 us: deliver(): lax.all_to_all(buffer, 'expert', split_axis=0, concat_axis=0, tiled=True)]
    unnamed x6 -> x4, waiting for transfers between devices: 163 us -> 163 us
  transfers between devices with their start and end apart: 6 -> 6, of which waited for: 5 -> 5; matrix products, arithmetic and copies ran while one was open for 10% -> 8% of each run, Pallas kernels for 0% -> 0%
where the time goes in v1:
time: 650 us; the launch traced here: 649 us
  waiting for transfers between devices  343 us (53%)
  blocking collectives  163 us (25%)
  matrix products  85.3 us (13%)
  starting transfers between devices  22.2 us (3%)
  local copies, waits for them, and re-layouts  19.1 us (3%)
  between operations  14.2 us (2%)
    all_to_all x1, waiting for transfers between devices, deliver(): lax.all_to_all(jnp.stack([arrived[None]] * lax.axis_size('fsdp')), 'fsdp'...  166 us
    unnamed x4, waiting for transfers between devices  163 us
    all_to_all x1, blocking collectives, deliver(): lax.all_to_all(jnp.stack([arrived[None]] * lax.axis_size('fsdp')), 'fsdp'...  147 us
    all_to_all x1, blocking collectives, deliver(): lax.all_to_all(buffer, 'expert', split_axis=0, concat_axis=0, tiled=True)  15.5 us
    dot_general x1, matrix products, per_device(): lax.dot_general(d_pre_up, w_up, contract_cols, preferred_element_type=jnp...  14.7 us
    another operation x2, local copies, waits for them, and re-layouts, deliver(): jnp.stack([arrived[None]] * lax.axis_size('fsdp'))  13.4 us
  transfers between devices with their start and end apart: 6, of which 5 were waited for; matrix products, arithmetic and copies ran while one was open for 8% of the time, Pallas kernels for 0%

profile of v1, /device:TPU:1, one launch (start us, length us, event | category | flops | bytes accessed | tf_op | source)
XLA Modules:
  0.0 649.2 jit_solution(12513221986421282020)
XLA Ops:
  7.2 0.9 copy.36
  8.1 0.1 reshape.105
  8.2 0.1 eq.62
  8.4 0.6 reduce-window.6
  8.9 0.2 slice_reduce_fusion
  9.2 0.1 fusion.17
  9.3 0.1 reduce_sum.42
  9.4 0.1 copy.38
  9.5 0.7 multiply_add_fusion
  10.3 0.6 copy-done.8
  10.9 2.2 convolution_convert_fusion.1
  13.1 5.8 all-to-all-start
  18.9 0.1 copy.40
  19.0 0.1 mul.83
  19.2 0.4 mul.85.clone
  19.6 1.1 mul.86
  20.7 0.5 convolution_convert_fusion.2
  21.1 10.0 %all-to-all-done = bf16[8,32,1536]{2,1,0:T(8,128)(2,1)} async-done(((bf16[8,32,1536]{2,1,0:T(8,128)(2,1)}), bf16[8,32,1536]{2,1,0:T(8,128)(2,1)}, u32[]{:S(2)}, u32[]{:S(2)}) %all-to-all-start) | async-done | bytes 786464 | tf_op jit(solution)/shard_map/all_to_all | solution.py:21
  31.2 15.5 %all_to_all.30 = bf16[8,32,1536]{2,1,0:T(8,128)(2,1)S(1)} all-to-all(bf16[8,32,1536]{2,1,0:T(8,128)(2,1)S(1)} %bitcast.68), channel_id=1, replica_groups=mesh['expert'=8,'fsdp'=16] {'expert'}, dimensions={0} | all-to-all | bytes 1572864 | tf_op jit(solution)/shard_map/all_to_all | solution.py:21
  46.7 7.3 %stack.6 = bf16[16,1,8,32,1536]{4,3,2,1,0:T(8,128)(2,1)} broadcast(bf16[8,32,1536]{2,1,0:T(8,128)(2,1)} %all-to-all-done), dimensions={2,3,4} | broadcast | bytes 13369344 | tf_op jit(solution)/shard_map/stack | solution.py:23
  53.9 147.4 %all_to_all.31 = bf16[16,1,8,32,1536]{4,3,2,1,0:T(8,128)(2,1)} all-to-all(bf16[16,1,8,32,1536]{4,3,2,1,0:T(8,128)(2,1)} %stack.6), channel_id=1, replica_groups=mesh['expert'=8,'fsdp'=16] {'fsdp'}, dimensions={0} | all-to-all | bytes 25165824 | tf_op jit(solution)/shard_map/all_to_all | solution.py:23
  201.4 6.1 stack.7
  207.5 5.1 all-to-all-start.4
  212.6 0.2 reduce-scatter.9.cloned.1.call-start
  212.9 7.8 %fusion.5 = f32[4096,128]{1,0:T(8,128)} fusion(bf16[4096,1536]{1,0:T(8,128)(2,1)} %bitcast.61, bf16[1,1536,128]{2,1,0:T(8,128)(2,1)S(1)} %copy-done.1), kind=kOutput, calls=%fused_computation.20 | convolution fusion | flops 1610612736 | bytes 15073280 | tf_op jit(solution)/shard_map/dot_general | solution.py:61
  220.7 7.8 %fusion.9 = f32[4096,128]{1,0:T(8,128)} fusion(bf16[4096,1536]{1,0:T(8,128)(2,1)} %bitcast.62, bf16[1,1536,128]{2,1,0:T(8,128)(2,1)S(1)} %copy-done.4), kind=kOutput, calls=%fused_computation.24 | convolution fusion | flops 1610612736 | bytes 15073280 | tf_op jit(solution)/shard_map/dot_general | solution.py:60
  228.4 165.8 %all-to-all-done.4 = bf16[16,1,8,32,1536]{4,3,2,1,0:T(8,128)(2,1)} async-done(((bf16[16,1,8,32,1536]{4,3,2,1,0:T(8,128)(2,1)}), bf16[16,1,8,32,1536]{4,3,2,1,0:T(8,128)(2,1)}, u32[]{:S(2)}, u32[]{:S(2)}) %all-to-all-start.4) | async-done | bytes 12582944 | tf_op jit(solution)/shard_map/all_to_all | solution.py:23
  394.3 9.6 %multiply_convert_fusion = (bf16[4096,128]{1,0:T(8,128)(2,1)S(1)}, bf16[4096,128]{1,0:T(8,128)(2,1)S(1)}, bf16[4096,128]{1,0:T(8,128)(2,1)S(1)}) fusion(f32[4096,128]{1,0:T(8,128)} %fusion.9, f32[4096,128]{1,0:T(8,128)} %fusion.5, bf16[4096,1536]{1,0:T(8,128)(2,1)} %bitcast.12, bf16[1,128,1536]{2,1,0:T(8,128)(2,1)S(1)} %copy-done), kind=kOutput, calls=%fused_computation.8 | convolution fusion | flops 1619001344 | bytes 20316160 | tf_op jit(solution)/shard_map/dot_general | solution.py:72
  403.9 10.1 %fusion.7 = f32[4096,1536]{1,0:T(8,128)} fusion(bf16[4096,128]{1,0:T(8,128)(2,1)S(1)} %get-tuple-element.9, bf16[1,1536,128]{2,1,0:T(8,128)(2,1)S(1)} %copy-done.4), kind=kOutput, calls=%fused_computation.22 | convolution fusion | flops 1610612736 | bytes 26607616 | tf_op jit(solution)/shard_map/dot_general | solution.py:82
  414.0 14.7 %add_convert_fusion = bf16[4096,1536]{1,0:T(8,128)(2,1)} fusion(f32[4096,1536]{1,0:T(8,128)} %fusion.7, bf16[4096,128]{1,0:T(8,128)(2,1)S(1)} %get-tuple-element.8, bf16[1,1536,128]{2,1,0:T(8,128)(2,1)S(1)} %copy-done.1), kind=kOutput, calls=%fused_computation | convolution fusion | flops 1623195648 | bytes 39190528 | tf_op jit(solution)/shard_map/dot_general | solution.py:85
  428.7 0.0 reduce-scatter.9.cloned.1.call-update
  428.8 0.3 reduce-scatter.7.cloned.1.call-start
  429.0 6.4 convolution_convert_fusion
  435.4 0.0 reduce-scatter.7.cloned.1.call-update
  435.4 1.0 copy-done.3
  436.4 1.0 convert_element_type.65
  437.3 0.1 iota_compare_fusion.2
  437.5 0.7 eq.68
  438.2 8.0 %convolution_bitcast_fusion.1 = f32[1,1536,128]{2,1,0:T(8,128)} fusion(bf16[4096,1536]{1,0:T(8,128)(2,1)} %bitcast.63, bf16[4096,128]{1,0:T(8,128)(2,1)S(1)} %get-tuple-element.8), kind=kOutput, calls=%fused_computation.5 | convolution fusion | flops 1610612736 | bytes 14417920 | tf_op jit(solution)/shard_map/dot_general | solution.py:81
  446.2 78.4 %reduce-scatter.9.cloned.1.call-done = bf16[1,8,32,1536]{3,2,1,0:T(8,128)(2,1)} async-done(((bf16[16,8,32,1536]{3,2,1,0:T(8,128)(2,1)}), bf16[1,8,32,1536]{3,2,1,0:T(8,128)(2,1)}) %reduce-scatter.9.cloned.1.call-update) | async-done | bytes 786448
  524.6 5.4 all-to-all-start.5
  530.0 7.3 %convolution_bitcast_fusion.2 = f32[1,1536,128]{2,1,0:T(8,128)} fusion(bf16[4096,1536]{1,0:T(8,128)(2,1)} %bitcast.64, bf16[4096,128]{1,0:T(8,128)(2,1)S(1)} %copy-done.6), kind=kOutput, calls=%fused_computation.6 | convolution fusion | flops 1610612736 | bytes 14417920 | tf_op jit(solution)/shard_map/dot_general | solution.py:78
  537.4 84.8 %reduce-scatter.7.cloned.1.call-done = bf16[1,8,32,1536]{3,2,1,0:T(8,128)(2,1)} async-done(((bf16[16,8,32,1536]{3,2,1,0:T(8,128)(2,1)}), bf16[1,8,32,1536]{3,2,1,0:T(8,128)(2,1)}) %reduce-scatter.7.cloned.1.call-update) | async-done | bytes 786448
  622.2 5.4 all-to-all-start.2
  627.6 7.4 %convolution_bitcast_fusion = f32[1,128,1536]{2,1,0:T(8,128)} fusion(bf16[4096,128]{1,0:T(8,128)(2,1)S(1)} %get-tuple-element.10, bf16[4096,1536]{1,0:T(8,128)(2,1)} %bitcast.12), kind=kOutput, calls=%fused_computation.4 | convolution fusion | flops 1610612736 | bytes 14417920 | tf_op jit(solution)/shard_map/dot_general | solution.py:77
  635.0 1.0 convolution_convert_fusion.3
  636.1 3.8 all-to-all-done.2
  639.9 2.5 multiply_reduce_fusion
  (28 shorter events, 0.1 us)
Async XLA Ops:
  7.2 387.1 %copy-start = (bf16[1,128,1536]{2,1,0:T(8,128)(2,1)S(1)}, bf16[1,128,1536]{2,1,0:T(8,128)(2,1)}, u32[]{:S(2)}) copy-start(bf16[1,128,1536]{2,1,0:T(8,128)(2,1)} %param.13) | copy-start | bytes 1179652
  7.2 11.7 %copy-start.11 = (f32[128,2]{0,1:T(2,128)S(1)}, f32[128,2]{0,1:T(2,128)}, u32[]{:S(2)}) copy-start(f32[128,2]{0,1:T(2,128)} %param.8) | copy-start | bytes 3076
  7.2 12.0 %copy-start.2 = (bf16[128,1536]{1,0:T(8,128)(2,1)S(1)}, bf16[128,1536]{1,0:T(8,128)(2,1)}, u32[]{:S(2)}) copy-start(bf16[128,1536]{1,0:T(8,128)(2,1)} %param.10) | copy-start | bytes 1179652
  10.2 0.6 copy-start.8
  13.1 18.1 %all-to-all-start = ((bf16[8,32,1536]{2,1,0:T(8,128)(2,1)}), bf16[8,32,1536]{2,1,0:T(8,128)(2,1)}, u32[]{:S(2)}, u32[]{:S(2)}) async-start(bf16[8,32,1536]{2,1,0:T(8,128)(2,1)} %bitcast.2), calls=%async_computation | async-start | bytes 1572864 | tf_op jit(solution)/shard_map/all_to_all | solution.py:21
  207.5 5.4 copy-start.1
  207.5 186.8 %all-to-all-start.4 = ((bf16[16,1,8,32,1536]{4,3,2,1,0:T(8,128)(2,1)}), bf16[16,1,8,32,1536]{4,3,2,1,0:T(8,128)(2,1)}, u32[]{:S(2)}, u32[]{:S(2)}) async-start(bf16[16,1,8,32,1536]{4,3,2,1,0:T(8,128)(2,1)} %stack.7), calls=%async_computation.4 | async-start | bytes 25165824 | tf_op jit(solution)/shard_map/all_to_all | solution.py:23
  212.6 312.0 %reduce-scatter.9.cloned.1.call-start = ((), (), s32[]{:S(2)}) async-start(), calls=%async_computation.9 | async-start | bytes 13369344
  212.9 7.8 %copy-start.4 = (bf16[1,1536,128]{2,1,0:T(8,128)(2,1)S(1)}, bf16[1,1536,128]{2,1,0:T(8,128)(2,1)}, u32[]{:S(2)}) copy-start(bf16[1,1536,128]{2,1,0:T(8,128)(2,1)} %param.11) | copy-start | bytes 1179652
  403.9 10.1 %copy-start.5 = (bf16[4096,128]{1,0:T(8,128)(2,1)}, bf16[4096,128]{1,0:T(8,128)(2,1)S(1)}, u32[]{:S(2)}) copy-start(bf16[4096,128]{1,0:T(8,128)(2,1)S(1)} %get-tuple-element.9) | copy-start | bytes 3145732
  428.8 193.4 %reduce-scatter.7.cloned.1.call-start = ((), (), s32[]{:S(2)}) async-start(), calls=%async_computation.8 | async-start | bytes 13369344
  435.4 1.0 copy-start.3
  438.2 91.8 %copy-start.6 = (bf16[4096,128]{1,0:T(8,128)(2,1)S(1)}, bf16[4096,128]{1,0:T(8,128)(2,1)}, u32[]{:S(2)}) copy-start(bf16[4096,128]{1,0:T(8,128)(2,1)} %copy-done.5) | copy-start | bytes 3145732
  524.6 97.6 %all-to-all-start.5 = ((bf16[8,32,1536]{2,1,0:T(8,128)(2,1)}), bf16[8,32,1536]{2,1,0:T(8,128)(2,1)S(1)}, u32[]{:S(2)}, u32[]{:S(2)}) async-start(bf16[8,32,1536]{2,1,0:T(8,128)(2,1)} %bitcast.70), calls=%async_computation.5 | async-start | bytes 1572864 | tf_op jit(solution)/shard_map/all_to_all | solution.py:32
  622.2 17.7 %all-to-all-start.2 = ((bf16[8,32,1536]{2,1,0:T(8,128)(2,1)}), bf16[8,32,1536]{2,1,0:T(8,128)(2,1)}, u32[]{:S(2)}, u32[]{:S(2)}) async-start(bf16[8,32,1536]{2,1,0:T(8,128)(2,1)} %bitcast.69), calls=%async_computation.2 | async-start | bytes 1572864 | tf_op jit(solution)/shard_map/all_to_all | solution.py:32
  627.6 7.4 %copy-start.9 = (bf16[256,128]{1,0:T(8,128)(2,1)S(1)}, bf16[256,128]{1,0:T(8,128)(2,1)}, u32[]{:S(2)}) copy-start(bf16[256,128]{1,0:T(8,128)(2,1)} %copy-done.8) | copy-start | bytes 196612
  627.6 12.3 %copy-start.7 = (f32[128,1536]{1,0:T(8,128)S(1)}, f32[128,1536]{1,0:T(8,128)}, u32[]{:S(2)}) copy-start(f32[128,1536]{1,0:T(8,128)} %convert_element_type.65) | copy-start | bytes 2359300
  627.6 12.3 %copy-start.10 = (pred[128,2,256]{2,1,0:T(4,128)(4,1)S(1)}, pred[128,2,256]{2,1,0:T(4,128)(4,1)}, u32[]{:S(2)}) copy-start(pred[128,2,256]{2,1,0:T(4,128)(4,1)} %eq.68) | copy-start | bytes 196612
Sparse Core Ops, SparseCore 0:
  428.9 95.6 reduce-scatter.8
  528.0 94.1 reduce-scatter.6
